TPU v7x, 1024 devices: a whole 4x4x32 slice. The times are simulated.
1024 devices in a mesh: dp: 4 (over x), ctx: 4 (over y_lo, core), exp: 64 (over z, y_hi).
Axes of the slice: x: 4, y: 4 (y_hi: 2, y_lo: 2; y = y_hi * 2 + y_lo), z: 32, core: 2. Of those that a mesh axis runs over, the one named last changes fastest.
Arguments:
- queries: bfloat16 [4, 1024, 3584], P('dp', 'ctx'), may hold values from -20 to 20
- keys: bfloat16 [4, 1024, 512], P('dp', 'ctx'), may hold values from -20 to 20
- values: bfloat16 [4, 1024, 512], P('dp', 'ctx'), may hold values from -6 to 6
- residual: bfloat16 [4, 1024, 3584], P('dp', 'ctx'), may hold values from -4 to 4
- labels: int32 [4, 8], P('dp'), may hold values from 0 to 1, as said below
- block_mask: int32 [4, 8, 8], P('dp'), may hold values from 0 to 1, as said below
- gains: float32 [2, 3584], replicated, may hold values from 0.5 to 1.5
- w_gate: bfloat16 [3584, 19456], P(None, 'exp'), may hold values from -0.09375 to 0.09375
- w_up: bfloat16 [3584, 19456], P(None, 'exp'), may hold values from -0.09375 to 0.09375
- w_down: bfloat16 [19456, 3584], P('exp'), may hold values from -0.15625 to 0.15625
Outputs:
- layer_out: bfloat16 [4, 1024, 3584], P('dp', ('ctx', 'exp'))
Inputs may be any that keep to these rules, and one draw needn't show every extreme that they name: `labels`: per sequence a share of visual blocks is drawn, then each block's label independently. Each sequence is packed with documents made of whole blocks, the first starting at block 0. block_mask[i, j] is 1 exactly when blocks i and j lie in the same document and (j <= i, or blocks i and j are both visual with no text block between them); the diagonal is always 1.
All inputs are finite; a program needn't handle non-finite values.
Results may differ from a plain program's by a relative error of at most 0.0069.
Values may be sent and summed in bfloat16 or wider, within the bound.
A program may use at most 64 MiB of HBM per device.

v0:
```python
import jax
import jax.numpy as jnp
from jax import lax
from jax.sharding import PartitionSpec as P

KV_HEADS = 4
HEAD_DIM = 128
BLOCK = 128


def per_device(queries, keys, values, residual, labels, block_mask, gains, w_gate, w_up, w_down):
    shard = queries.shape[1]
    width = queries.shape[2]
    group = width // (KV_HEADS * HEAD_DIM)
    head_width = group * HEAD_DIM
    exp_count = lax.axis_size("exp")
    exp_here = lax.axis_index("exp")
    slices = exp_count // KV_HEADS
    rows_sub = shard // slices
    slice_id = exp_here // KV_HEADS
    head_id = exp_here % KV_HEADS
    shard_base = lax.axis_index("ctx") * shard
    labels_row = labels[0]
    block_count = labels_row.shape[0]
    block_ids = jnp.arange(block_count, dtype=jnp.int32)
    labels_float = labels_row.astype(jnp.float32)
    mask_float = block_mask[0].astype(jnp.float32)
    q_first = slice_id * rows_sub
    q_local = lax.dynamic_slice(
        queries[0], (q_first, head_id * head_width), (rows_sub, head_width)
    ).reshape(rows_sub, group, HEAD_DIM)
    q_pos = shard_base + q_first + jnp.arange(rows_sub, dtype=jnp.int32)
    q_blk = q_pos // BLOCK
    q_onehot = (q_blk[:, None] == block_ids[None, :]).astype(jnp.float32)
    q_mask_rows = jnp.dot(q_onehot, mask_float)
    q_visual = jnp.dot(q_onehot, labels_float)
    scale = 1.0 / jnp.sqrt(jnp.float32(HEAD_DIM))
    whole_keys, whole_values = (
        lax.all_gather(keys, "ctx", axis=1, tiled=True),
        lax.all_gather(values, "ctx", axis=1, tiled=True),
    )
    count = whole_keys.shape[1]
    k_head = lax.dynamic_slice_in_dim(whole_keys[0], head_id * HEAD_DIM, HEAD_DIM, 1)
    v_head = lax.dynamic_slice_in_dim(whole_values[0], head_id * HEAD_DIM, HEAD_DIM, 1)
    k_pos = jnp.arange(count, dtype=jnp.int32)
    k_blk = k_pos // BLOCK
    k_onehot = (block_ids[:, None] == k_blk[None, :]).astype(jnp.float32)
    block_ok = jnp.dot(q_mask_rows, k_onehot) > 0.5
    allowed = block_ok & (
        (k_blk[None, :] != q_blk[:, None])
        | (k_pos[None, :] <= q_pos[:, None])
        | (q_visual[:, None] > 0.5)
    )
    scores = jnp.einsum("qrd,kd->rqk", q_local, k_head, preferred_element_type=jnp.float32) * scale
    scores = jnp.where(allowed[None], scores, -1e30)
    run_max = jnp.full((group, rows_sub), -1e30, jnp.float32)
    new_max = jnp.maximum(run_max, jnp.max(scores, axis=-1))
    weights = jnp.where(allowed[None], jnp.exp(scores - new_max[..., None]), 0.0)
    total = jnp.sum(weights, axis=-1)
    soft = weights.astype(jnp.bfloat16)
    accum = jnp.einsum("rqk,kd->rqd", soft, v_head, preferred_element_type=jnp.float32)
    attended = accum / total[..., None]
    own_part = jnp.transpose(attended, (1, 0, 2)).reshape(rows_sub, head_width).astype(jnp.bfloat16)
    collected = lax.all_gather(own_part[None], "exp", axis=0, tiled=True)
    attention = jnp.transpose(
        collected.reshape(slices, KV_HEADS, rows_sub, head_width), (0, 2, 1, 3)
    ).reshape(shard, width)
    mid = residual[0].astype(jnp.float32) + attention.astype(jnp.float32)
    row_blk = (shard_base + jnp.arange(shard, dtype=jnp.int32)) // BLOCK
    row_visual = jnp.dot((row_blk[:, None] == block_ids[None, :]).astype(jnp.float32), labels_float)
    gain_rows = jnp.where(row_visual[:, None] > 0.5, gains[1][None, :], gains[0][None, :])
    normed = (
        mid * lax.rsqrt(jnp.mean(mid * mid, axis=-1, keepdims=True) + 1e-05) * gain_rows
    ).astype(jnp.bfloat16)
    section = (exp_here >= exp_count // 2).astype(jnp.float32)
    keep = (row_visual == section).astype(jnp.float32)
    gate = jnp.dot(normed, w_gate, preferred_element_type=jnp.float32)
    upper = jnp.dot(normed, w_up, preferred_element_type=jnp.float32)
    hidden = (jax.nn.silu(gate) * upper).astype(jnp.bfloat16)
    partial_terms = jnp.dot(hidden, w_down, preferred_element_type=jnp.float32) * keep[:, None]
    branch = lax.psum_scatter(partial_terms[None], "exp", scatter_dimension=1, tiled=True)
    out_rows = shard // exp_count
    mid_rows = lax.dynamic_slice_in_dim(mid, exp_here * out_rows, out_rows, 0)
    return (mid_rows[None] + branch).astype(jnp.bfloat16)


def solution(mesh):
    placed = (
        P("dp", "ctx", None),
        P("dp", "ctx", None),
        P("dp", "ctx", None),
        P("dp", "ctx", None),
        P("dp", None),
        P("dp", None, None),
        P(),
        P(None, "exp"),
        P(None, "exp"),
        P("exp", None),
    )
    return jax.shard_map(
        per_device,
        mesh=mesh,
        in_specs=placed,
        out_specs=P("dp", ("ctx", "exp"), None),
        check_vma=False,
    )
```

profile of v0, /device:TPU:4, one launch (start us, length us, event | category | flops | bytes accessed | tf_op | source)
XLA Modules:
  0.0 1012.9 jit_solution(17143297318540550657)
XLA Ops:
  6.5 0.0 copy-start
  6.5 0.0 copy-start.6
  6.5 0.0 copy-start.4
  6.5 0.0 all-gather.4.cloned.1.call-start
  6.5 0.7 all-gather.4.cloned.1.call-update
  7.3 0.0 all-gather.6.cloned.1.call-start
  7.3 0.7 all-gather.6.cloned.1.call-update
  8.0 0.0 all-gather.8.cloned.1.call-start
  8.1 0.8 constant_dynamic-slice_fusion
  8.9 0.1 reshape.100
  9.0 0.8 fusion.9
  9.8 1.1 fusion.6
  10.9 45.2 %all-gather.4.cloned.1.call-done = bf16[1,1024,512]{2,1,0:T(8,128)(2,1)} async-done(((bf16[1,256,512]{2,1,0:T(8,128)(2,1)}), bf16[1,1024,512]{2,1,0:T(8,128)(2,1)}) %all-gather.4.cloned.1.call-update) | async-done | bytes 1048592 | tf_op jit(solution)/shard_map/all_gather | solution.py:39
  56.1 1.2 fusion.47
  57.4 0.2 fusion.10
  57.6 41.0 %all-gather.6.cloned.1.call-done = bf16[1,1024,512]{2,1,0:T(8,128)(2,1)} async-done(((bf16[1,256,512]{2,1,0:T(8,128)(2,1)}), bf16[1,1024,512]{2,1,0:T(8,128)(2,1)}) %all-gather.6.cloned.1.call-update) | async-done | bytes 1048592 | tf_op jit(solution)/shard_map/all_gather | solution.py:40
  98.6 1.2 fusion.5
  99.8 0.7 convert_element_type.72
  100.5 0.0 all-gather.8.cloned.1.call-update
  100.5 0.0 all-reduce.3.cloned.1.call-start
  100.6 0.0 copy-done.4
  100.6 0.1 slice_reduce_fusion.1
  100.7 0.0 copy-done.6
  100.7 0.2 fusion.26
  100.9 278.4 %all-gather.8.cloned.1.call-done = bf16[64,16,896]{2,1,0:T(8,128)(2,1)} async-done(((bf16[1,16,896]{2,1,0:T(8,128)(2,1)}), bf16[64,16,896]{2,1,0:T(8,128)(2,1)}) %all-gather.8.cloned.1.call-update) | async-done | bytes 1835024 | tf_op jit(solution)/shard_map/all_gather | solution.py:64
  379.3 1.9 convert_bitcast_fusion
  381.2 1.4 copy.18
  382.6 0.0 copy-start.3
  382.6 0.2 copy.21
  382.9 1.2 copy-done.3
  384.1 0.9 multiply_reduce_fusion
  385.0 0.0 copy-start.1
  385.0 0.0 copy-start.5
  385.0 0.7 multiply_convert_fusion
  385.7 1.2 copy-done.1
  386.9 1.1 copy-done.5
  388.0 0.0 copy-start.2
  388.0 0.8 fusion.48
  388.7 0.5 copy-done.2
  389.2 0.0 copy-done
  389.2 7.1 fusion
  396.3 0.0 all-reduce.3.cloned.1.call-update
  396.4 1.3 dynamic-slice.3
  398.3 606.5 %all-reduce.3.cloned.1.call-done = f32[1,256,3584]{2,1,0:T(8,128)} async-done(((f32[1,256,3584]{2,1,0:T(8,128)}), f32[1,256,3584]{2,1,0:T(8,128)}) %all-reduce.3.cloned.1.call-update) | async-done | bytes 3670032
  1004.8 1.6 fusion.30
  (7 shorter events, 0.1 us)
Async XLA Ops:
  6.5 382.7 %copy-start = (bf16[304,3584]{1,0:T(8,128)(2,1)S(1)}, bf16[304,3584]{1,0:T(8,128)(2,1)}, u32[]{:S(2)}) copy-start(bf16[304,3584]{1,0:T(8,128)(2,1)} %param.19) | copy-start | bytes 6537220
  6.5 94.1 %copy-start.6 = (s32[1,8]{1,0:T(1,128)S(1)}, s32[1,8]{1,0:T(1,128)}, u32[]{:S(2)}) copy-start(s32[1,8]{1,0:T(1,128)} %param.14) | copy-start | bytes 100
  6.5 94.1 %copy-start.4 = (f32[2,3584]{1,0:T(2,128)S(1)}, f32[2,3584]{1,0:T(2,128)}, u32[]{:S(2)}) copy-start(f32[2,3584]{1,0:T(2,128)} %param.16) | copy-start | bytes 86020
  6.5 49.6 %all-gather.4.cloned.1.call-start = ((), (), s32[]{:S(2)}) async-start(), calls=%async_computation | async-start | bytes 1310720 | tf_op jit(solution)/shard_map/all_gather | solution.py:39
  7.3 91.3 %all-gather.6.cloned.1.call-start = ((), (), s32[]{:S(2)}) async-start(), calls=%async_computation.1 | async-start | bytes 1310720 | tf_op jit(solution)/shard_map/all_gather | solution.py:40
  8.0 371.3 %all-gather.8.cloned.1.call-start = ((), (), s32[]{:S(2)}) async-start(), calls=%async_computation.2 | async-start | bytes 1863680 | tf_op jit(solution)/shard_map/all_gather | solution.py:64
  100.5 904.2 %all-reduce.3.cloned.1.call-start = ((), (), s32[]{:S(2)}) async-start(), calls=%async_computation.3 | async-start | bytes 7340032
  382.6 1.5 copy-start.3
  385.0 1.9 copy-start.1
  385.0 2.9 copy-start.5
  388.0 1.2 copy-start.2
Sparse Core Ops, SparseCore 0:
  10.0 46.0 all-gather.3
  58.8 39.7 all-gather.5
  102.8 276.4 all-gather.7
  396.5 608.2 all-reduce.2
where the time goes:
time: 1010 us
  waiting for transfers between devices  973 us (96%)
  between operations  14 us (1%)
  matrix products  12.5 us (1%)
    unnamed x5, waiting for transfers between devices  608 us
    all_gather x1, waiting for transfers between devices, per_device(): collected = lax.all_gather(own_part[None], 'exp', axis=0, tiled=True)  278 us
    all_gather x1, waiting for transfers between devices, per_device(): lax.all_gather(keys, 'ctx', axis=1, tiled=True)  45.2 us
    all_gather x1, waiting for transfers between devices, per_device(): lax.all_gather(values, 'ctx', axis=1, tiled=True)  41 us
  transfers between devices with their start and end apart: 4, of which 4 were waited for; matrix products, arithmetic and copies ran while one was open for 1% of the time, Pallas kernels for 0%

commit v1 on v0

v1 whole, which is shorter than its diff:
```python
import functools
import math

import jax
import jax.numpy as jnp
from jax import lax
from jax.experimental import pallas as pl
from jax.experimental.pallas import tpu as pltpu
from jax.sharding import PartitionSpec as P

KV_HEADS = 4
HEAD_DIM = 128
BLOCK = 128
NEG = -1e30
MESH = pl.DeviceIdType.MESH
PIECES = 2
STREAMS = 2
ANY = pl.BlockSpec(memory_space=pl.ANY)
VMEM = pl.BlockSpec(memory_space=pltpu.VMEM)
SMEM = pl.BlockSpec(memory_space=pltpu.SMEM)


def kv_kernel(k_ref, v_ref, ko_ref, vo_ref, lsem, ssem, rsem):
    rows = k_ref.shape[0]
    piece = rows // PIECES
    c = lax.axis_index("ctx")
    e = lax.axis_index("exp")
    sib = c + 1 - 2 * (c % 2)
    oth = (c + 2) % 4
    twin = e + 1 - 2 * (e % 2)
    barrier = pltpu.get_barrier_semaphore()
    for dev in ({"ctx": sib}, {"ctx": oth}, {"ctx": oth, "exp": twin}):
        pl.semaphore_signal(barrier, inc=1, device_id=dev, device_id_type=MESH)
    pl.semaphore_wait(barrier, 3)

    def rows_at(shard, i, size):
        return pl.ds(pl.multiple_of(shard * rows + i * size, size), size)

    cross, started = [], []
    for i in range(PIECES):
        for kind, (src, dst, dev) in enumerate(
            ((k_ref, ko_ref, {"ctx": oth}), (v_ref, vo_ref, {"ctx": oth, "exp": twin}))
        ):
            copy = pltpu.make_async_remote_copy(
                src_ref=src.at[pl.ds(i * piece, piece)],
                dst_ref=dst.at[rows_at(c, i, piece)],
                send_sem=ssem.at[kind, i],
                recv_sem=rsem.at[kind, i],
                device_id=dev,
                device_id_type=MESH,
            )
            copy.start()
            cross.append(copy)
    for kind, (src, dst) in enumerate(((k_ref, ko_ref), (v_ref, vo_ref))):
        copy = pltpu.make_async_remote_copy(
            src_ref=src,
            dst_ref=dst.at[rows_at(c, 0, rows)],
            send_sem=ssem.at[2 + kind, 0],
            recv_sem=rsem.at[2 + kind, 0],
            device_id={"ctx": sib},
            device_id_type=MESH,
        )
        copy.start()
        started.append(copy)
    local = []
    for kind, (src, dst) in enumerate(((k_ref, ko_ref), (v_ref, vo_ref))):
        copy = pltpu.make_async_copy(src, dst.at[rows_at(c, 0, rows)], lsem.at[kind])
        copy.start()
        local.append(copy)
    for i in range(PIECES):
        for kind, dst in enumerate((ko_ref, vo_ref)):
            cross[2 * i + kind].wait_recv()
            copy = pltpu.make_async_remote_copy(
                src_ref=dst.at[rows_at(oth, i, piece)],
                dst_ref=dst.at[rows_at(oth, i, piece)],
                send_sem=ssem.at[4 + kind, i],
                recv_sem=rsem.at[4 + kind, i],
                device_id={"ctx": sib},
                device_id_type=MESH,
            )
            copy.start()
            started.append(copy)
    for copy in started:
        copy.wait_recv()
    for copy in cross + started:
        copy.wait_send()
    for copy in local:
        copy.wait()


def kv_exchange(keys, values):
    rows, width = keys.shape
    whole = jax.ShapeDtypeStruct((4 * rows, width), keys.dtype)
    return pl.pallas_call(
        kv_kernel,
        out_shape=(whole, whole),
        in_specs=[ANY, ANY],
        out_specs=(ANY, ANY),
        scratch_shapes=[
            pltpu.SemaphoreType.DMA((2,)),
            pltpu.SemaphoreType.DMA((6, PIECES)),
            pltpu.SemaphoreType.DMA((6, PIECES)),
        ],
        compiler_params=pltpu.CompilerParams(collective_id=0, has_side_effects=True),
        name="kv_exchange",
    )(keys, values)


def layer_kernel(
    label_ref, mask_ref, q_ref, k_ref, v_ref, res_ref, gain_ref, wg_any, wu_any, wd_any,
    part_ref, own_ref, bias, mid, normed, wg, wu, wd, sems,
):
    rows, width = q_ref.shape
    count = k_ref.shape[0]
    heads = width // HEAD_DIM
    group = heads // KV_HEADS
    here = rows // BLOCK
    copies = [
        pltpu.make_async_copy(src, dst, sems.at[i])
        for i, (src, dst) in enumerate(((wg_any, wg), (wu_any, wu), (wd_any, wd)))
    ]
    for copy in copies:
        copy.start()
    first = lax.axis_index("ctx") * here
    e = lax.axis_index("exp")
    exp_count = lax.axis_size("exp")
    causal = lax.broadcasted_iota(jnp.int32, (BLOCK, BLOCK), 1) <= lax.broadcasted_iota(
        jnp.int32, (BLOCK, BLOCK), 0
    )
    for b in range(here):
        q_blk = first + b
        for j in range(count // BLOCK):
            sees = mask_ref[q_blk, j] == 1
            whole = sees & ((q_blk != j) | (label_ref[q_blk] == 1))
            upper = jnp.where(whole, 0.0, NEG)
            lower = jnp.where(sees, 0.0, NEG)
            bias[b * BLOCK:(b + 1) * BLOCK, j * BLOCK:(j + 1) * BLOCK] = jnp.where(causal, lower, upper)
    factor = math.log2(math.e) / math.sqrt(HEAD_DIM)

    def head(h, squares):
        at = pl.ds(pl.multiple_of(h * HEAD_DIM, HEAD_DIM), HEAD_DIM)
        kv_at = pl.ds(pl.multiple_of((h // group) * HEAD_DIM, HEAD_DIM), HEAD_DIM)
        scores = lax.dot_general(
            q_ref[:, at], k_ref[:, kv_at], (((1,), (1,)), ((), ())), preferred_element_type=jnp.float32
        ) + bias[...]
        top = jnp.max(scores, axis=-1, keepdims=True)
        weights = jnp.exp2((scores - top) * factor)
        total = jnp.sum(weights, axis=-1, keepdims=True)
        mixed = jnp.dot(weights.astype(jnp.bfloat16), v_ref[:, kv_at], preferred_element_type=jnp.float32)
        x = res_ref[:, at].astype(jnp.float32) + (mixed / total).astype(jnp.bfloat16).astype(jnp.float32)
        mid[:, at] = x
        return squares + x * x

    squares = lax.fori_loop(0, heads, head, jnp.zeros((rows, HEAD_DIM), jnp.float32))
    inverse = lax.rsqrt(jnp.sum(squares, axis=-1, keepdims=True) / width + 1e-05)
    for b in range(here):
        at = slice(b * BLOCK, (b + 1) * BLOCK)
        visual = label_ref[first + b] == 1
        gain = jnp.where(visual, gain_ref[1:2, :], gain_ref[0:1, :])
        normed[at, :] = (mid[at, :] * inverse[at] * gain).astype(jnp.bfloat16)
    slot = rows // (exp_count // 2)
    own_ref[...] = mid[pl.ds(pl.multiple_of((e // 2) * slot, slot), slot), :]
    for copy in copies:
        copy.wait()
    x = normed[...]
    last = (((1,), (1,)), ((), ()))
    gate = lax.dot_general(x, wg[...], last, preferred_element_type=jnp.float32)
    upper = lax.dot_general(x, wu[...], last, preferred_element_type=jnp.float32)
    hidden = (jax.nn.silu(gate) * upper).astype(jnp.bfloat16)
    section = jnp.where(e >= exp_count // 2, 1, 0)
    tile = 512
    for t in range(width // tile):
        cols = slice(t * tile, (t + 1) * tile)
        out = jnp.dot(hidden, wd[:, cols], preferred_element_type=jnp.float32)
        for b in range(here):
            keep = label_ref[first + b] == section
            kept = jnp.where(keep, out[b * BLOCK:(b + 1) * BLOCK], 0.0)
            part_ref[b * (BLOCK // slot):(b + 1) * (BLOCK // slot), :, cols] = kept.reshape(
                BLOCK // slot, slot, tile
            ).astype(jnp.bfloat16)


def layer(labels, mask, q, k, v, res, gains, wg, wu, wd, exp_count):
    rows, width = q.shape
    hidden = wg.shape[0]
    slots = exp_count // 2
    slot = rows // slots
    return pl.pallas_call(
        layer_kernel,
        out_shape=(
            jax.ShapeDtypeStruct((slots, slot, width), jnp.bfloat16),
            jax.ShapeDtypeStruct((slot, width), jnp.float32),
        ),
        in_specs=[SMEM, SMEM, VMEM, VMEM, VMEM, VMEM, VMEM, ANY, ANY, ANY],
        out_specs=(VMEM, VMEM),
        scratch_shapes=[
            pltpu.VMEM((rows, k.shape[0]), jnp.float32),
            pltpu.VMEM((rows, width), jnp.float32),
            pltpu.VMEM((rows, width), jnp.bfloat16),
            pltpu.VMEM((hidden, width), jnp.bfloat16),
            pltpu.VMEM((hidden, width), jnp.bfloat16),
            pltpu.VMEM((hidden, width), jnp.bfloat16),
            pltpu.SemaphoreType.DMA((3,)),
        ],
        compiler_params=pltpu.CompilerParams(vmem_limit_bytes=48 * 1024 * 1024),
        name="layer",
    )(labels, mask, q, k, v, res, gains, wg, wu, wd)


def reduce_kernel(slots, part_ref, mid_ref, out_ref, up_buf, dn_buf, tw_in, tw_out, ssem, rsem, tsem):
    width = part_ref.shape[2]
    cols = width // STREAMS
    half = slots // 2
    e = lax.axis_index("exp")
    z = e // 2
    count = 2 * slots
    up = (e + 2) % count
    dn = (e + count - 2) % count
    twin = e + 1 - 2 * (e % 2)
    barrier = pltpu.get_barrier_semaphore()
    for dev in (up, dn, twin):
        pl.semaphore_signal(barrier, inc=1, device_id={"exp": dev}, device_id_type=MESH)
    pl.semaphore_wait(barrier, 3)

    def hop(way, src, step, t):
        buf = (up_buf, dn_buf)[way]
        return pltpu.make_async_remote_copy(
            src_ref=src,
            dst_ref=buf.at[step, :, pl.ds(t * cols, cols)],
            send_sem=ssem.at[way, step, t],
            recv_sem=rsem.at[way, step, t],
            device_id={"exp": (up, dn)[way]},
            device_id_type=MESH,
        )

    def slot_of(way, step):
        if way == 0:
            return (z + half - 1 - step + slots) % slots
        return (z + half + step) % slots

    for t in range(STREAMS):
        for way in range(2):
            hop(way, part_ref.at[slot_of(way, 0), :, pl.ds(t * cols, cols)], 0, t).start()

    def advance(way, step, t):
        buf = (up_buf, dn_buf)[way]
        at = pl.ds(t * cols, cols)
        src = buf.at[step - 1, :, at]
        hop(way, src, step - 1, t).wait_recv()
        own = part_ref[slot_of(way, step), :, at]
        buf[step - 1, :, at] = (buf[step - 1, :, at].astype(jnp.float32) + own.astype(jnp.float32)).astype(
            jnp.bfloat16
        )
        hop(way, src, step, t).start()

    def both(step, carry):
        for t in range(STREAMS):
            for way in range(2):
                advance(way, step, t)
        return carry

    lax.fori_loop(1, half - 1, both, 0)
    for t in range(STREAMS):
        advance(1, half - 1, t)
    for t in range(STREAMS):
        at = pl.ds(t * cols, cols)
        hop(0, up_buf.at[half - 2, :, at], half - 2, t).wait_recv()
        hop(1, dn_buf.at[half - 1, :, at], half - 1, t).wait_recv()
    mine = (
        part_ref[z].astype(jnp.float32)
        + up_buf[half - 2].astype(jnp.float32)
        + dn_buf[half - 1].astype(jnp.float32)
    )
    tw_out[...] = mine.astype(jnp.bfloat16)
    swap = pltpu.make_async_remote_copy(
        src_ref=tw_out, dst_ref=tw_in, send_sem=tsem.at[0], recv_sem=tsem.at[1],
        device_id={"exp": twin}, device_id_type=MESH,
    )
    swap.start()
    swap.wait_recv()
    total = mid_ref[...] + (mine + tw_in[...].astype(jnp.float32))
    size = total.shape[0] // 2
    picked = jnp.where(e % 2 == 0, total[:size], total[size:])
    out_ref[...] = picked.astype(jnp.bfloat16)
    swap.wait_send()

    def drain(step, carry):
        for t in range(STREAMS):
            for way in range(2):
                hop(way, part_ref.at[0, :, pl.ds(t * cols, cols)], step, t).wait_send()
        return carry

    lax.fori_loop(0, half - 1, drain, 0)
    for t in range(STREAMS):
        hop(1, part_ref.at[0, :, pl.ds(t * cols, cols)], half - 1, t).wait_send()


def reduce_parts(part, mid):
    slots, slot, width = part.shape
    half = slots // 2
    return pl.pallas_call(
        functools.partial(reduce_kernel, slots),
        out_shape=jax.ShapeDtypeStruct((slot // 2, width), jnp.bfloat16),
        in_specs=[VMEM, VMEM],
        out_specs=VMEM,
        scratch_shapes=[
            pltpu.VMEM((half, slot, width), jnp.bfloat16),
            pltpu.VMEM((half, slot, width), jnp.bfloat16),
            pltpu.VMEM((slot, width), jnp.bfloat16),
            pltpu.VMEM((slot, width), jnp.bfloat16),
            pltpu.SemaphoreType.DMA((2, half, STREAMS)),
            pltpu.SemaphoreType.DMA((2, half, STREAMS)),
            pltpu.SemaphoreType.DMA((2,)),
        ],
        compiler_params=pltpu.CompilerParams(collective_id=1, has_side_effects=True),
        name="reduce_parts",
    )(part, mid)


def per_device(queries, keys, values, residual, labels, block_mask, gains, w_gate, w_up, w_down):
    whole_keys, whole_values = kv_exchange(keys[0], values[0])
    part, own = layer(
        labels[0], block_mask[0], queries[0], whole_keys, whole_values, residual[0], gains,
        w_gate.T, w_up.T, w_down, lax.axis_size("exp"),
    )
    return reduce_parts(part, own)[None]


def solution(mesh):
    placed = (
        P("dp", "ctx", None),
        P("dp", "ctx", None),
        P("dp", "ctx", None),
        P("dp", "ctx", None),
        P("dp", None),
        P("dp", None, None),
        P(),
        P(None, "exp"),
        P(None, "exp"),
        P("exp", None),
    )
    return jax.shard_map(
        per_device,
        mesh=mesh,
        in_specs=placed,
        out_specs=P("dp", ("ctx", "exp"), None),
        check_vma=False,
    )
```

time: 1010 us -> 132 us (0.13)
  waiting for transfers between devices: 973 us -> 0 us
  Pallas kernels: 0 us -> 122 us
  between operations: 14 us -> 0.05 us
  matrix products: 12.5 us -> 0 us
    unnamed x5 -> x0, waiting for transfers between devices: 608 us -> none
    all_gather x3 -> x0, waiting for transfers between devices: 365 us -> none  [the longest x1 278 us: per_device(): collected = lax.all_gather(own_part[None], 'exp', axis=0, tiled=True)]
    pallas_call x0 -> x3, Pallas kernels: none -> 122 us  [the longest x1 77.2 us: reduce_parts(): pl.pallas_call(functools.partial(reduce_kernel, slots), out_shape=jax.Sha...]
    dot_general x7 -> x0, matrix products: 12.5 us -> none  [the longest x1 7.1 us: per_device(): jnp.dot(hidden, w_down, preferred_element_type=jnp.float32) * keep[:, None]]
  transfers between devices with their start and end apart: 4 -> 0, of which waited for: 4 -> 0; matrix products, arithmetic and copies ran while one was open for 1% -> 0% of each run, Pallas kernels for 0% -> 0%
where the time goes in v1:
time: 132 us
  Pallas kernels  122 us (92%)
  local copies, waits for them, and re-layouts  9.28 us (7%)
    pallas_call x1, Pallas kernels, reduce_parts(): pl.pallas_call(functools.partial(reduce_kernel, slots), out_shape=jax.Sha...  77.2 us
    pallas_call x1, Pallas kernels, layer(): pl.pallas_call(layer_kernel, out_shape=(jax.ShapeDtypeStruct((slots, slot...  24 us
    pallas_call x1, Pallas kernels, kv_exchange(): pl.pallas_call(kv_kernel, out_shape=(whole, whole), in_specs=[ANY, ANY],...  21 us
    unnamed x17, local copies, waits for them, and re-layouts  9.28 us

profile of v1, /device:TPU:4, one launch (start us, length us, event | category | flops | bytes accessed | tf_op | source)
XLA Modules:
  0.0 131.5 jit_solution(14421315033000933530)
XLA Ops:
  0.0 21.0 %kv_exchange.1 = (bf16[1024,512]{1,0:T(8,128)(2,1)}, bf16[1024,512]{1,0:T(8,128)(2,1)}) custom-call(bf16[256,512]{1,0:T(8,128)(2,1)} %bitcast.15, bf16[256,512]{1,0:T(8,128)(2,1)} %bitcast.16), custom_call_target="tpu_custom_call" | custom-call | tf_op jit(solution)/shard_map/kv_exchange/pallas_call | solution.py:94
  21.0 0.0 copy-start
  21.0 1.5 %copy-done = bf16[1,256,3584]{2,1,0:T(8,128)(2,1)S(1)} copy-done((bf16[1,256,3584]{2,1,0:T(8,128)(2,1)S(1)}, bf16[1,256,3584]{2,1,0:T(8,128)(2,1)}, u32[]{:S(2)}) %copy-start) | copy-done | bytes 1835032
  22.5 0.0 copy-start.2
  22.5 1.2 copy-done.2
  23.7 0.0 copy-start.3
  23.7 1.2 copy-done.3
  25.0 0.0 copy-start.5
  25.0 0.7 copy-done.5
  25.7 0.0 copy-start.6
  25.7 0.7 copy-done.6
  26.4 0.0 copy-start.7
  26.4 0.7 copy-done.7
  27.0 24.0 %layer.1 = (bf16[32,8,3584]{2,1,0:T(8,128)(2,1)S(1)}, f32[8,3584]{1,0:T(8,128)S(1)}) custom-call(s32[8]{0:T(128)S(1)} %bitcast.11, s32[8,8]{1,0:T(8,128)S(1)} %bitcast.10, bf16[256,3584]{1,0:T(8,128)(2,1)S(1)} %bitcast.9, bf16[1024,512]{1,0:T(8,128)(2,1)S(1)} %copy-done.2, bf16[1024,512]{1,0:T(8,128)(2,1)S(1)} %copy-done.3, bf16[256,3584]{1,0:T(8,128)(2,1)} %bitcast.14, ...), custom_call_target="tpu_custom_call" | custom-call | tf_op jit(solution)/shard_map/layer/pallas_call | solution.py:188
  51.1 0.0 copy-start.1
  51.1 1.2 copy-done.1
  52.3 0.0 copy-start.4
  52.3 0.6 copy-done.4
  52.9 77.2 %reduce_parts.1 = bf16[4,3584]{1,0:T(4,128)(2,1)} custom-call(bf16[32,8,3584]{2,1,0:T(8,128)(2,1)} %copy-done.1, f32[8,3584]{1,0:T(8,128)} %copy-done.4), custom_call_target="tpu_custom_call" | custom-call | tf_op jit(solution)/shard_map/reduce_parts/pallas_call | solution.py:301
  130.2 1.4 %copy.12 = bf16[1,4,3584]{2,1,0:T(4,128)(2,1)} copy(bf16[1,4,3584]{2,1,0:T(4,128)(2,1)} %bitcast.17) | data formatting | bytes 57344
Async XLA Ops:
  21.0 1.5 %copy-start = (bf16[1,256,3584]{2,1,0:T(8,128)(2,1)S(1)}, bf16[1,256,3584]{2,1,0:T(8,128)(2,1)}, u32[]{:S(2)}) copy-start(bf16[1,256,3584]{2,1,0:T(8,128)(2,1)} %param.10) | copy-start | bytes 5505028
  22.5 1.2 copy-start.2
  23.7 1.2 copy-start.3
  25.0 0.7 copy-start.5
  25.7 0.7 copy-start.6
  26.4 0.7 copy-start.7
  51.1 1.2 copy-start.1
  52.3 0.6 copy-start.4

commit v2 on v1

v2 whole, which is shorter than its diff:
```python
import functools
import math

import jax
import jax.numpy as jnp
from jax import lax
from jax.experimental import pallas as pl
from jax.experimental.pallas import tpu as pltpu
from jax.sharding import PartitionSpec as P

KV_HEADS = 4
HEAD_DIM = 128
BLOCK = 128
NEG = -1e30
MESH = pl.DeviceIdType.MESH
PIECES = 2
STREAMS = 4
ANY = pl.BlockSpec(memory_space=pl.ANY)
VMEM = pl.BlockSpec(memory_space=pltpu.VMEM)
SMEM = pl.BlockSpec(memory_space=pltpu.SMEM)


def kv_kernel(k_ref, v_ref, ko_ref, vo_ref, lsem, ssem, rsem):
    rows = k_ref.shape[0]
    piece = rows // PIECES
    c = lax.axis_index("ctx")
    e = lax.axis_index("exp")
    sib = c + 1 - 2 * (c % 2)
    oth = (c + 2) % 4
    twin = e + 1 - 2 * (e % 2)
    barrier = pltpu.get_barrier_semaphore()
    for dev in ({"ctx": sib}, {"ctx": oth}, {"ctx": oth, "exp": twin}):
        pl.semaphore_signal(barrier, inc=1, device_id=dev, device_id_type=MESH)
    pl.semaphore_wait(barrier, 3)

    def rows_at(shard, i, size):
        return pl.ds(pl.multiple_of(shard * rows + i * size, size), size)

    cross, started = [], []
    for i in range(PIECES):
        for kind, (src, dst, dev) in enumerate(
            ((k_ref, ko_ref, {"ctx": oth}), (v_ref, vo_ref, {"ctx": oth, "exp": twin}))
        ):
            copy = pltpu.make_async_remote_copy(
                src_ref=src.at[pl.ds(i * piece, piece)],
                dst_ref=dst.at[rows_at(c, i, piece)],
                send_sem=ssem.at[kind, i],
                recv_sem=rsem.at[kind, i],
                device_id=dev,
                device_id_type=MESH,
            )
            copy.start()
            cross.append(copy)
    for kind, (src, dst) in enumerate(((k_ref, ko_ref), (v_ref, vo_ref))):
        copy = pltpu.make_async_remote_copy(
            src_ref=src,
            dst_ref=dst.at[rows_at(c, 0, rows)],
            send_sem=ssem.at[2 + kind, 0],
            recv_sem=rsem.at[2 + kind, 0],
            device_id={"ctx": sib},
            device_id_type=MESH,
        )
        copy.start()
        started.append(copy)
    local = []
    for kind, (src, dst) in enumerate(((k_ref, ko_ref), (v_ref, vo_ref))):
        copy = pltpu.make_async_copy(src, dst.at[rows_at(c, 0, rows)], lsem.at[kind])
        copy.start()
        local.append(copy)
    for i in range(PIECES):
        for kind, dst in enumerate((ko_ref, vo_ref)):
            cross[2 * i + kind].wait_recv()
            copy = pltpu.make_async_remote_copy(
                src_ref=dst.at[rows_at(oth, i, piece)],
                dst_ref=dst.at[rows_at(oth, i, piece)],
                send_sem=ssem.at[4 + kind, i],
                recv_sem=rsem.at[4 + kind, i],
                device_id={"ctx": sib},
                device_id_type=MESH,
            )
            copy.start()
            started.append(copy)
    for copy in started:
        copy.wait_recv()
    for copy in cross + started:
        copy.wait_send()
    for copy in local:
        copy.wait()


def kv_exchange(keys, values):
    rows, width = keys.shape
    whole = jax.ShapeDtypeStruct((4 * rows, width), keys.dtype)
    return pl.pallas_call(
        kv_kernel,
        out_shape=(whole, whole),
        in_specs=[ANY, ANY],
        out_specs=(ANY, ANY),
        scratch_shapes=[
            pltpu.SemaphoreType.DMA((2,)),
            pltpu.SemaphoreType.DMA((6, PIECES)),
            pltpu.SemaphoreType.DMA((6, PIECES)),
        ],
        compiler_params=pltpu.CompilerParams(collective_id=0, has_side_effects=True),
        name="kv_exchange",
    )(keys, values)


def chains(slots):
    half = slots // 2
    near = half // 2
    return ((1, half - 1, near + 1), (-1, half, near + 1), (1, near, 1), (-1, near, 1))


def layer_kernel(
    slots, label_ref, mask_ref, gain_ref, q_any, k_any, v_any, res_any, wg_any, wu_any, wd_any,
    out_ref, q_ref, k_ref, v_ref, res_ref, bias, mid, normed, wg, wu, wd, part,
    buf, fin, tw_in, tw_out, lsem, ssem, rsem, tsem,
):
    rows, width = q_ref.shape
    count = k_ref.shape[0]
    heads = width // HEAD_DIM
    group = heads // KV_HEADS
    here = rows // BLOCK
    slot = rows // slots
    cols = width // STREAMS
    first = lax.axis_index("ctx") * here
    e = lax.axis_index("exp")
    z = e // 2
    twin = e + 1 - 2 * (e % 2)
    plan = chains(slots)
    reach = plan[0][2]

    def along(distance):
        return (e + 2 * (distance + slots)) % (2 * slots)

    barrier = pltpu.get_barrier_semaphore()
    partners = [along(1), along(-1), along(reach), along(-reach), twin]
    for dev in partners:
        pl.semaphore_signal(barrier, inc=1, device_id={"exp": dev}, device_id_type=MESH)
    loads = [
        pltpu.make_async_copy(src, dst, lsem.at[i])
        for i, (src, dst) in enumerate(
            (
                (q_any, q_ref), (k_any, k_ref), (v_any, v_ref), (res_any, res_ref),
                (wg_any, wg), (wu_any, wu), (wd_any, wd),
            )
        )
    ]
    for load in loads:
        load.start()
    causal = lax.broadcasted_iota(jnp.int32, (BLOCK, BLOCK), 1) <= lax.broadcasted_iota(
        jnp.int32, (BLOCK, BLOCK), 0
    )
    for b in range(here):
        q_blk = first + b
        for j in range(count // BLOCK):
            sees = mask_ref[q_blk, j] == 1
            whole = sees & ((q_blk != j) | (label_ref[q_blk] == 1))
            upper = jnp.where(whole, 0.0, NEG)
            lower = jnp.where(sees, 0.0, NEG)
            bias[b * BLOCK:(b + 1) * BLOCK, j * BLOCK:(j + 1) * BLOCK] = jnp.where(causal, lower, upper)
    for load in loads[:4]:
        load.wait()
    factor = math.log2(math.e) / math.sqrt(HEAD_DIM)

    def head(h, squares):
        at = pl.ds(pl.multiple_of(h * HEAD_DIM, HEAD_DIM), HEAD_DIM)
        kv_at = pl.ds(pl.multiple_of((h // group) * HEAD_DIM, HEAD_DIM), HEAD_DIM)
        scores = lax.dot_general(
            q_ref[:, at], k_ref[:, kv_at], (((1,), (1,)), ((), ())), preferred_element_type=jnp.float32
        ) + bias[...]
        top = jnp.max(scores, axis=-1, keepdims=True)
        weights = jnp.exp2((scores - top) * factor)
        total = jnp.sum(weights, axis=-1, keepdims=True)
        mixed = jnp.dot(weights.astype(jnp.bfloat16), v_ref[:, kv_at], preferred_element_type=jnp.float32)
        x = res_ref[:, at].astype(jnp.float32) + (mixed / total).astype(jnp.bfloat16).astype(jnp.float32)
        mid[:, at] = x
        return squares + x * x

    squares = lax.fori_loop(0, heads, head, jnp.zeros((rows, HEAD_DIM), jnp.float32))
    inverse = lax.rsqrt(jnp.sum(squares, axis=-1, keepdims=True) / width + 1e-05)
    for b in range(here):
        at = slice(b * BLOCK, (b + 1) * BLOCK)
        visual = label_ref[first + b] == 1
        gain = jnp.where(visual, gain_ref[1:2, :], gain_ref[0:1, :])
        normed[at, :] = (mid[at, :] * inverse[at] * gain).astype(jnp.bfloat16)
    for load in loads[4:]:
        load.wait()
    x = normed[...]
    last = (((1,), (1,)), ((), ()))
    gate = lax.dot_general(x, wg[...], last, preferred_element_type=jnp.float32)
    upper = lax.dot_general(x, wu[...], last, preferred_element_type=jnp.float32)
    hidden = (jax.nn.silu(gate) * upper).astype(jnp.bfloat16)
    pl.semaphore_wait(barrier, len(partners))

    def hop(i, step, t, src):
        way, farthest, nearest = plan[i]
        final = isinstance(step, int) and step == farthest - nearest
        at = pl.ds(t * cols, cols)
        return pltpu.make_async_remote_copy(
            src_ref=src,
            dst_ref=fin.at[i, :, at] if final else buf.at[i, step, :, at],
            send_sem=ssem.at[i, step, t],
            recv_sem=rsem.at[i, step, t],
            device_id={"exp": along(way * nearest if final else way)},
            device_id_type=MESH,
        )

    def chunk(i, step):
        way, farthest, _ = plan[i]
        return (z + way * (farthest - step) + 2 * slots) % slots

    def advance(i, step, t):
        at = pl.ds(t * cols, cols)
        src = buf.at[i, step - 1, :, at]
        hop(i, step - 1, t, src).wait_recv()
        own = part[chunk(i, step), :, at]
        buf[i, step - 1, :, at] = (buf[i, step - 1, :, at].astype(jnp.float32) + own.astype(jnp.float32)).astype(
            jnp.bfloat16
        )
        hop(i, step, t, src).start()

    section = jnp.where(e >= slots, 1, 0)
    tile = width // 4
    for u in range(4):
        span = slice(u * tile, (u + 1) * tile)
        out = jnp.dot(hidden, wd[:, span], preferred_element_type=jnp.float32)
        for b in range(here):
            keep = label_ref[first + b] == section
            kept = jnp.where(keep, out[b * BLOCK:(b + 1) * BLOCK], 0.0)
            part[b * (BLOCK // slot):(b + 1) * (BLOCK // slot), :, span] = kept.reshape(
                BLOCK // slot, slot, tile
            ).astype(jnp.bfloat16)
        for t in range(STREAMS):
            if (u + 1) * STREAMS == 4 * (t + 1):
                for i in range(len(plan)):
                    hop(i, 0, t, part.at[chunk(i, 0), :, pl.ds(t * cols, cols)]).start()

    lengths = [farthest - nearest + 1 for _, farthest, nearest in plan]
    same = min(lengths) - 1

    def step_all(step, carry):
        for t in range(STREAMS):
            for i in range(len(plan)):
                advance(i, step, t)
        return carry

    if same > 1:
        lax.fori_loop(1, same, step_all, 0)
    for step in range(max(same, 1), max(lengths)):
        for t in range(STREAMS):
            for i in range(len(plan)):
                if step < lengths[i]:
                    advance(i, step, t)
    mine = part[z].astype(jnp.float32)
    for i in (2, 3, 0, 1):
        for t in range(STREAMS):
            at = pl.ds(t * cols, cols)
            hop(i, lengths[i] - 1, t, fin.at[i, :, at]).wait_recv()
        mine = mine + fin[i].astype(jnp.float32)
    tw_out[...] = mine.astype(jnp.bfloat16)
    swap = pltpu.make_async_remote_copy(
        src_ref=tw_out, dst_ref=tw_in, send_sem=tsem.at[0], recv_sem=tsem.at[1],
        device_id={"exp": twin}, device_id_type=MESH,
    )
    swap.start()
    swap.wait_recv()
    total = mid[pl.ds(pl.multiple_of(z * slot, slot), slot), :] + (mine + tw_in[...].astype(jnp.float32))
    size = slot // 2
    out_ref[...] = jnp.where(e % 2 == 0, total[:size], total[size:]).astype(jnp.bfloat16)
    swap.wait_send()
    for i in range(len(plan)):
        for step in range(lengths[i]):
            for t in range(STREAMS):
                hop(i, step, t, part.at[0, :, pl.ds(t * cols, cols)]).wait_send()


def layer(labels, mask, q, k, v, res, gains, wg, wu, wd, exp_count):
    rows, width = q.shape
    hidden = wg.shape[0]
    slots = exp_count // 2
    slot = rows // slots
    steps = slots // 4
    half = jnp.bfloat16
    return pl.pallas_call(
        functools.partial(layer_kernel, slots),
        out_shape=jax.ShapeDtypeStruct((slot // 2, width), half),
        in_specs=[SMEM, SMEM, VMEM, ANY, ANY, ANY, ANY, ANY, ANY, ANY],
        out_specs=VMEM,
        scratch_shapes=[
            pltpu.VMEM((rows, width), half),
            pltpu.VMEM(k.shape, half),
            pltpu.VMEM(v.shape, half),
            pltpu.VMEM((rows, width), half),
            pltpu.VMEM((rows, k.shape[0]), jnp.float32),
            pltpu.VMEM((rows, width), jnp.float32),
            pltpu.VMEM((rows, width), half),
            pltpu.VMEM((hidden, width), half),
            pltpu.VMEM((hidden, width), half),
            pltpu.VMEM((hidden, width), half),
            pltpu.VMEM((slots, slot, width), half),
            pltpu.VMEM((4, steps, slot, width), half),
            pltpu.VMEM((4, slot, width), half),
            pltpu.VMEM((slot, width), half),
            pltpu.VMEM((slot, width), half),
            pltpu.SemaphoreType.DMA((7,)),
            pltpu.SemaphoreType.DMA((4, steps, STREAMS)),
            pltpu.SemaphoreType.DMA((4, steps, STREAMS)),
            pltpu.SemaphoreType.DMA((2,)),
        ],
        compiler_params=pltpu.CompilerParams(
            vmem_limit_bytes=58 * 1024 * 1024, collective_id=1, has_side_effects=True
        ),
        name="layer",
    )(labels, mask, gains, q, k, v, res, wg, wu, wd)


def per_device(queries, keys, values, residual, labels, block_mask, gains, w_gate, w_up, w_down):
    whole_keys, whole_values = kv_exchange(keys[0], values[0])
    out = layer(
        labels[0], block_mask[0], queries[0], whole_keys, whole_values, residual[0], gains,
        w_gate.T, w_up.T, w_down, lax.axis_size("exp"),
    )
    return out[None]


def solution(mesh):
    placed = (
        P("dp", "ctx", None),
        P("dp", "ctx", None),
        P("dp", "ctx", None),
        P("dp", "ctx", None),
        P("dp", None),
        P("dp", None, None),
        P(),
        P(None, "exp"),
        P(None, "exp"),
        P("exp", None),
    )
    return jax.shard_map(
        per_device,
        mesh=mesh,
        in_specs=placed,
        out_specs=P("dp", ("ctx", "exp"), None),
        check_vma=False,
    )
```

time: 132 us -> 108 us (0.82)
  the two profiles are of different devices: /device:TPU:4 before, /device:TPU:96 now
where the time goes in v2:
time: 108 us; the launch traced here: 107 us
  Pallas kernels  106 us (98%)
  local copies, waits for them, and re-layouts  1.37 us (1%)
    pallas_call x1, Pallas kernels, layer(): pl.pallas_call(functools.partial(layer_kernel, slots), out_shape=jax.Shap...  84.9 us
    pallas_call x1, Pallas kernels, kv_exchange(): pl.pallas_call(kv_kernel, out_shape=(whole, whole), in_specs=[ANY, ANY],...  21 us

profile of v2, /device:TPU:96, one launch (start us, length us, event | category | flops | bytes accessed | tf_op | source)
XLA Modules:
  0.0 107.3 jit_solution(10488244005487226886)
XLA Ops:
  0.0 21.0 %kv_exchange.1 = (bf16[1024,512]{1,0:T(8,128)(2,1)}, bf16[1024,512]{1,0:T(8,128)(2,1)}) custom-call(bf16[256,512]{1,0:T(8,128)(2,1)} %bitcast.13, bf16[256,512]{1,0:T(8,128)(2,1)} %bitcast.14), custom_call_target="tpu_custom_call" | custom-call | tf_op jit(solution)/shard_map/kv_exchange/pallas_call | solution.py:94
  21.0 84.9 %layer.1 = bf16[4,3584]{1,0:T(4,128)(2,1)} custom-call(s32[8]{0:T(128)} %bitcast.17, s32[8,8]{1,0:T(8,128)} %bitcast.16, f32[2,3584]{1,0:T(2,128)} %gain_ref.1, bf16[256,3584]{1,0:T(8,128)(2,1)} %bitcast.11, bf16[1024,512]{1,0:T(8,128)(2,1)} %get-tuple-element.7.k_any, bf16[1024,512]{1,0:T(8,128)(2,1)} %get-tuple-element.8.v_any, ...), custom_call_target="tpu_custom_call" | custom-call | tf_op jit(solution)/shard_map/layer/pallas_call | solution.py:286
  105.9 1.4 %copy.12 = bf16[1,4,3584]{2,1,0:T(4,128)(2,1)} copy(bf16[1,4,3584]{2,1,0:T(4,128)(2,1)} %bitcast.15) | data formatting | bytes 57344

commit v3 on v2

v3 whole, which is shorter than its diff:
```python
import functools
import math

import jax
import jax.numpy as jnp
from jax import lax
from jax.experimental import pallas as pl
from jax.experimental.pallas import tpu as pltpu
from jax.sharding import PartitionSpec as P

KV_HEADS = 4
HEAD_DIM = 128
BLOCK = 128
NEG = -1e30
MESH = pl.DeviceIdType.MESH
STREAMS = 4
ANY = pl.BlockSpec(memory_space=pl.ANY)
VMEM = pl.BlockSpec(memory_space=pltpu.VMEM)
SMEM = pl.BlockSpec(memory_space=pltpu.SMEM)


def chains(slots):
    half = slots // 2
    near = half // 2
    return ((1, half - 1, near + 1), (-1, half, near + 1), (1, near, 1), (-1, near, 1))


def layer_kernel(
    slots, label_ref, mask_ref, gain_ref, q_any, k_any, v_any, res_any, wg_any, wu_any, wd_any,
    out_ref, q_ref, kv_ref, res_ref, bias, tops, sums, mid, normed, wg, wu, wd, part,
    buf, fin, tw_in, tw_out, lsem, ksem, kssem, krsem, ssem, rsem, tsem, known,
):
    rows, width = q_ref.shape
    count = kv_ref.shape[2]
    heads = width // HEAD_DIM
    group = heads // KV_HEADS
    here = rows // BLOCK
    slot = rows // slots
    cols = width // STREAMS
    c = lax.axis_index("ctx")
    first = c * here
    e = lax.axis_index("exp")
    z = e // 2
    twin = e + 1 - 2 * (e % 2)
    sib = c + 1 - 2 * (c % 2)
    oth = (c + 2) % 4
    plan = chains(slots)
    reach = plan[0][2]

    def along(distance):
        return (e + 2 * (distance + slots)) % (2 * slots)

    barrier = pltpu.get_barrier_semaphore()
    partners = [{"exp": along(1)}, {"exp": along(-1)}, {"exp": twin}, {"ctx": sib}, {"ctx": oth}]
    partners.append({"ctx": oth, "exp": twin})
    for dev in partners:
        pl.semaphore_signal(barrier, inc=1, device_id=dev, device_id_type=MESH)
    own_loads = [
        pltpu.make_async_copy(
            src.at[:, pl.ds(g * HEAD_DIM, HEAD_DIM)], kv_ref.at[kind, g, pl.ds(0, rows)], ksem.at[kind, g]
        )
        for g in range(KV_HEADS)
        for kind, src in enumerate((k_any, v_any))
    ]
    loads = [
        pltpu.make_async_copy(src, dst, lsem.at[i])
        for i, (src, dst) in enumerate(
            ((q_any, q_ref), (res_any, res_ref), (wg_any, wg), (wu_any, wu), (wd_any, wd))
        )
    ]
    for load in own_loads + loads:
        load.start()
    causal = lax.broadcasted_iota(jnp.int32, (BLOCK, BLOCK), 1) <= lax.broadcasted_iota(
        jnp.int32, (BLOCK, BLOCK), 0
    )
    for b in range(here):
        q_blk = first + b
        for r, shard in enumerate((c, sib, oth, sib + 2 - 4 * (sib // 2))):
            for j in range(here):
                sees = mask_ref[q_blk, shard * here + j] == 1
                lower = jnp.where(sees, 0.0, NEG)
                if r == 0 and j == b:
                    upper = jnp.where(sees & (label_ref[q_blk] == 1), 0.0, NEG)
                    square = jnp.where(causal, lower, upper)
                else:
                    square = jnp.full((BLOCK, BLOCK), lower, jnp.float32)
                at = r * rows + j * BLOCK
                bias[b * BLOCK:(b + 1) * BLOCK, at:at + BLOCK] = square
    for load in own_loads:
        load.wait()

    def piece(stage, kind, g):
        source, target, dev = (
            (0, 2, {"ctx": oth, "exp": twin} if kind else {"ctx": oth}),
            (0, 1, {"ctx": sib}),
            (2, 3, {"ctx": sib}),
        )[stage]
        return pltpu.make_async_remote_copy(
            src_ref=kv_ref.at[kind, g, pl.ds(source * rows, rows)],
            dst_ref=kv_ref.at[kind, g, pl.ds(target * rows, rows)],
            send_sem=kssem.at[stage, kind, g],
            recv_sem=krsem.at[stage, kind, g],
            device_id=dev,
            device_id_type=MESH,
        )

    pl.semaphore_wait(barrier, len(partners))
    for stage in range(2):
        for g in range(KV_HEADS):
            for kind in range(2):
                piece(stage, kind, g).start()

    def tell(i, distance):
        for way in (distance, -distance):
            pl.semaphore_signal(known.at[i], inc=1, device_id={"exp": along(way)}, device_id_type=MESH)

    def learn(i):
        pl.semaphore_wait(known.at[i], 2)

    hops = [1]
    distance = 2
    while distance * 2 <= reach:
        hops.append(distance)
        distance *= 2
    hops += [1] * (reach - distance)
    tell(0, hops[0])
    for load in loads[:2]:
        load.wait()
    factor = math.log2(math.e) / math.sqrt(HEAD_DIM)

    def place(h):
        return pl.ds(pl.multiple_of(h * HEAD_DIM, HEAD_DIM), HEAD_DIM)

    def scores_of(h, g, span):
        return lax.dot_general(
            q_ref[:, place(h)], kv_ref[0, g, span], (((1,), (1,)), ((), ())), preferred_element_type=jnp.float32
        ) + bias[:, span]

    def begin(h, carry):
        g = h // group
        scores = scores_of(h, g, slice(0, rows))
        top = jnp.max(scores, axis=-1, keepdims=True)
        weights = jnp.exp2((scores - top) * factor)
        tops[h] = top
        sums[h] = jnp.sum(weights, axis=-1, keepdims=True)
        mid[:, place(h)] = jnp.dot(
            weights.astype(jnp.bfloat16), kv_ref[1, g, 0:rows], preferred_element_type=jnp.float32
        )
        return carry

    lax.fori_loop(0, heads, begin, 0)

    def finish(g, h, squares):
        rest = slice(rows, count)
        scores = scores_of(h, g, rest)
        old = tops[h]
        top = jnp.maximum(old, jnp.max(scores, axis=-1, keepdims=True))
        weights = jnp.exp2((scores - top) * factor)
        shrink = jnp.exp2((old - top) * factor)
        total = sums[h] * shrink + jnp.sum(weights, axis=-1, keepdims=True)
        mixed = mid[:, place(h)] * shrink + jnp.dot(
            weights.astype(jnp.bfloat16), kv_ref[1, g, rest], preferred_element_type=jnp.float32
        )
        x = res_ref[:, place(h)].astype(jnp.float32) + (mixed / total).astype(jnp.bfloat16).astype(jnp.float32)
        mid[:, place(h)] = x
        return squares + x * x

    def forward(g):
        for kind in range(2):
            piece(0, kind, g).wait_recv()
            piece(2, kind, g).start()

    forward(0)
    squares = jnp.zeros((rows, HEAD_DIM), jnp.float32)
    for g in range(KV_HEADS):
        if g + 1 < KV_HEADS:
            forward(g + 1)
        for stage in (1, 2):
            for kind in range(2):
                piece(stage, kind, g).wait_recv()
        if g < len(hops):
            learn(g)
            if g + 1 < len(hops):
                tell(g + 1, hops[g + 1])
        squares = lax.fori_loop(g * group, (g + 1) * group, functools.partial(finish, g), squares)
    inverse = lax.rsqrt(jnp.sum(squares, axis=-1, keepdims=True) / width + 1e-05)
    for b in range(here):
        at = slice(b * BLOCK, (b + 1) * BLOCK)
        visual = label_ref[first + b] == 1
        gain = jnp.where(visual, gain_ref[1:2, :], gain_ref[0:1, :])
        normed[at, :] = (mid[at, :] * inverse[at] * gain).astype(jnp.bfloat16)
    for load in loads[2:]:
        load.wait()
    x = normed[...]
    last = (((1,), (1,)), ((), ()))
    gate = lax.dot_general(x, wg[...], last, preferred_element_type=jnp.float32)
    upper = lax.dot_general(x, wu[...], last, preferred_element_type=jnp.float32)
    hidden = (jax.nn.silu(gate) * upper).astype(jnp.bfloat16)

    def hop(i, step, t, src):
        way, farthest, nearest = plan[i]
        final = isinstance(step, int) and step == farthest - nearest
        at = pl.ds(t * cols, cols)
        return pltpu.make_async_remote_copy(
            src_ref=src,
            dst_ref=fin.at[i, :, at] if final else buf.at[i, step, :, at],
            send_sem=ssem.at[i, step, t],
            recv_sem=rsem.at[i, step, t],
            device_id={"exp": along(way * nearest if final else way)},
            device_id_type=MESH,
        )

    def chunk(i, step):
        way, farthest, _ = plan[i]
        return (z + way * (farthest - step) + 2 * slots) % slots

    def advance(i, step, t):
        at = pl.ds(t * cols, cols)
        src = buf.at[i, step - 1, :, at]
        hop(i, step - 1, t, src).wait_recv()
        own = part[chunk(i, step), :, at]
        buf[i, step - 1, :, at] = (buf[i, step - 1, :, at].astype(jnp.float32) + own.astype(jnp.float32)).astype(
            jnp.bfloat16
        )
        hop(i, step, t, src).start()

    section = jnp.where(e >= slots, 1, 0)
    tile = width // 4
    for u in range(4):
        span = slice(u * tile, (u + 1) * tile)
        out = jnp.dot(hidden, wd[:, span], preferred_element_type=jnp.float32)
        for b in range(here):
            keep = label_ref[first + b] == section
            kept = jnp.where(keep, out[b * BLOCK:(b + 1) * BLOCK], 0.0)
            part[b * (BLOCK // slot):(b + 1) * (BLOCK // slot), :, span] = kept.reshape(
                BLOCK // slot, slot, tile
            ).astype(jnp.bfloat16)
        for t in range(STREAMS):
            if (u + 1) * STREAMS == 4 * (t + 1):
                for i in range(len(plan)):
                    hop(i, 0, t, part.at[chunk(i, 0), :, pl.ds(t * cols, cols)]).start()

    lengths = [farthest - nearest + 1 for _, farthest, nearest in plan]
    same = min(lengths) - 1

    def step_all(step, carry):
        for t in range(STREAMS):
            for i in range(len(plan)):
                advance(i, step, t)
        return carry

    if same > 1:
        lax.fori_loop(1, same, step_all, 0)
    for step in range(max(same, 1), max(lengths)):
        for t in range(STREAMS):
            for i in range(len(plan)):
                if step < lengths[i]:
                    advance(i, step, t)
    mine = part[z].astype(jnp.float32)
    for i in (2, 3, 0, 1):
        for t in range(STREAMS):
            at = pl.ds(t * cols, cols)
            hop(i, lengths[i] - 1, t, fin.at[i, :, at]).wait_recv()
        mine = mine + fin[i].astype(jnp.float32)
    tw_out[...] = mine.astype(jnp.bfloat16)
    swap = pltpu.make_async_remote_copy(
        src_ref=tw_out, dst_ref=tw_in, send_sem=tsem.at[0], recv_sem=tsem.at[1],
        device_id={"exp": twin}, device_id_type=MESH,
    )
    swap.start()
    swap.wait_recv()
    total = mid[pl.ds(pl.multiple_of(z * slot, slot), slot), :] + (mine + tw_in[...].astype(jnp.float32))
    size = slot // 2
    out_ref[...] = jnp.where(e % 2 == 0, total[:size], total[size:]).astype(jnp.bfloat16)
    swap.wait_send()
    for stage in range(3):
        for kind in range(2):
            for g in range(KV_HEADS):
                piece(stage, kind, g).wait_send()
    for i in range(len(plan)):
        for step in range(lengths[i]):
            for t in range(STREAMS):
                hop(i, step, t, part.at[0, :, pl.ds(t * cols, cols)]).wait_send()


def layer(labels, mask, q, k, v, res, gains, wg, wu, wd, exp_count):
    rows, width = q.shape
    hidden = wg.shape[0]
    slots = exp_count // 2
    slot = rows // slots
    steps = slots // 4
    count = 4 * rows
    half = jnp.bfloat16
    return pl.pallas_call(
        functools.partial(layer_kernel, slots),
        out_shape=jax.ShapeDtypeStruct((slot // 2, width), half),
        in_specs=[SMEM, SMEM, VMEM, ANY, ANY, ANY, ANY, ANY, ANY, ANY],
        out_specs=VMEM,
        scratch_shapes=[
            pltpu.VMEM((rows, width), half),
            pltpu.VMEM((2, KV_HEADS, count, HEAD_DIM), half),
            pltpu.VMEM((rows, width), half),
            pltpu.VMEM((rows, count), jnp.float32),
            pltpu.VMEM((width // HEAD_DIM, rows, 1), jnp.float32),
            pltpu.VMEM((width // HEAD_DIM, rows, 1), jnp.float32),
            pltpu.VMEM((rows, width), jnp.float32),
            pltpu.VMEM((rows, width), half),
            pltpu.VMEM((hidden, width), half),
            pltpu.VMEM((hidden, width), half),
            pltpu.VMEM((hidden, width), half),
            pltpu.VMEM((slots, slot, width), half),
            pltpu.VMEM((4, steps, slot, width), half),
            pltpu.VMEM((4, slot, width), half),
            pltpu.VMEM((slot, width), half),
            pltpu.VMEM((slot, width), half),
            pltpu.SemaphoreType.DMA((5,)),
            pltpu.SemaphoreType.DMA((2, KV_HEADS)),
            pltpu.SemaphoreType.DMA((3, 2, KV_HEADS)),
            pltpu.SemaphoreType.DMA((3, 2, KV_HEADS)),
            pltpu.SemaphoreType.DMA((4, steps, STREAMS)),
            pltpu.SemaphoreType.DMA((4, steps, STREAMS)),
            pltpu.SemaphoreType.DMA((2,)),
            pltpu.SemaphoreType.REGULAR((KV_HEADS,)),
        ],
        compiler_params=pltpu.CompilerParams(
            vmem_limit_bytes=58 * 1024 * 1024, collective_id=1, has_side_effects=True
        ),
        name="layer",
    )(labels, mask, gains, q, k, v, res, wg, wu, wd)


def per_device(queries, keys, values, residual, labels, block_mask, gains, w_gate, w_up, w_down):
    out = layer(
        labels[0], block_mask[0], queries[0], keys[0], values[0], residual[0], gains,
        w_gate.T, w_up.T, w_down, lax.axis_size("exp"),
    )
    return out[None]


def solution(mesh):
    placed = (
        P("dp", "ctx", None),
        P("dp", "ctx", None),
        P("dp", "ctx", None),
        P("dp", "ctx", None),
        P("dp", None),
        P("dp", None, None),
        P(),
        P(None, "exp"),
        P(None, "exp"),
        P("exp", None),
    )
    return jax.shard_map(
        per_device,
        mesh=mesh,
        in_specs=placed,
        out_specs=P("dp", ("ctx", "exp"), None),
        check_vma=False,
    )
```

time: 108 us -> 107 us (level)
  the two profiles are of different devices: /device:TPU:96 before, /device:TPU:98 now
where the time goes in v3:
time: 107 us; the launch traced here: 106 us
  Pallas kernels  105 us (98%)
  local copies, waits for them, and re-layouts  1.37 us (1%)
    pallas_call x1, Pallas kernels, layer(): pl.pallas_call(functools.partial(layer_kernel, slots), out_shape=jax.Shap...  105 us

profile of v3, /device:TPU:98, one launch (start us, length us, event | category | flops | bytes accessed | tf_op | source)
XLA Modules:
  0.0 106.3 jit_solution(2500732006008662204)
XLA Ops:
  0.0 104.9 %layer.1 = bf16[4,3584]{1,0:T(4,128)(2,1)} custom-call(s32[8]{0:T(128)} %bitcast.17, s32[8,8]{1,0:T(8,128)} %bitcast.16, f32[2,3584]{1,0:T(2,128)} %gain_ref.1, bf16[256,3584]{1,0:T(8,128)(2,1)} %bitcast.11, bf16[256,512]{1,0:T(8,128)(2,1)} %bitcast.13, bf16[256,512]{1,0:T(8,128)(2,1)} %bitcast.14, bf16[256,3584]{1,0:T(8,128)(2,1)} %bitcast.12, ...), custom_call_target="tpu_custom_call" | custom-call | tf_op jit(solution)/shard_map/layer/pallas_call | solution.py:294
  104.9 1.4 %copy.12 = bf16[1,4,3584]{2,1,0:T(4,128)(2,1)} copy(bf16[1,4,3584]{2,1,0:T(4,128)(2,1)} %bitcast.15) | data formatting | bytes 57344

commit v4 on v3

--- a/solution.py
+++ b/solution.py
@@ -21,7 +21,7 @@
 
 def chains(slots):
     half = slots // 2
-    near = half // 2
+    near = half // 2 + half // 16
     return ((1, half - 1, near + 1), (-1, half, near + 1), (1, near, 1), (-1, near, 1))
 
 
@@ -117,12 +117,10 @@
     def learn(i):
         pl.semaphore_wait(known.at[i], 2)
 
-    hops = [1]
-    distance = 2
-    while distance * 2 <= reach:
-        hops.append(distance)
-        distance *= 2
-    hops += [1] * (reach - distance)
+    hops, distance = [], 1
+    while distance < reach:
+        hops.append(min(distance, reach - distance))
+        distance += hops[-1]
     tell(0, hops[0])
     for load in loads[:2]:
         load.wait()
@@ -148,7 +146,7 @@
         )
         return carry
 
-    lax.fori_loop(0, heads, begin, 0)
+    lax.fori_loop(0, heads, begin, 0, unroll=4)
 
     def finish(g, h, squares):
         rest = slice(rows, count)
@@ -182,7 +180,7 @@
             learn(g)
             if g + 1 < len(hops):
                 tell(g + 1, hops[g + 1])
-        squares = lax.fori_loop(g * group, (g + 1) * group, functools.partial(finish, g), squares)
+        squares = lax.fori_loop(g * group, (g + 1) * group, functools.partial(finish, g), squares, unroll=group)
     inverse = lax.rsqrt(jnp.sum(squares, axis=-1, keepdims=True) / width + 1e-05)
     for b in range(here):
         at = slice(b * BLOCK, (b + 1) * BLOCK)
@@ -288,7 +286,7 @@
     hidden = wg.shape[0]
     slots = exp_count // 2
     slot = rows // slots
-    steps = slots // 4
+    steps = max(farthest - nearest + 1 for _, farthest, nearest in chains(slots))
     count = 4 * rows
     half = jnp.bfloat16
     return pl.pallas_call(

time: 107 us -> 96.3 us (0.900)
  the two profiles are of different devices: /device:TPU:98 before, /device:TPU:70 now
where the time goes in v4:
time: 96.3 us; the launch traced here: 96.1 us
  Pallas kernels  94.7 us (98%)
  local copies, waits for them, and re-layouts  1.37 us (1%)
    pallas_call x1, Pallas kernels, layer(): pl.pallas_call(functools.partial(layer_kernel, slots), out_shape=jax.Shap...  94.7 us

profile of v4, /device:TPU:70, one launch (start us, length us, event | category | flops | bytes accessed | tf_op | source)
XLA Modules:
  0.0 96.1 jit_solution(348533955310766286)
XLA Ops:
  0.0 94.7 %layer.1 = bf16[4,3584]{1,0:T(4,128)(2,1)} custom-call(s32[8]{0:T(128)} %bitcast.17, s32[8,8]{1,0:T(8,128)} %bitcast.16, f32[2,3584]{1,0:T(2,128)} %gain_ref.1, bf16[256,3584]{1,0:T(8,128)(2,1)} %bitcast.11, bf16[256,512]{1,0:T(8,128)(2,1)} %bitcast.13, bf16[256,512]{1,0:T(8,128)(2,1)} %bitcast.14, bf16[256,3584]{1,0:T(8,128)(2,1)} %bitcast.12, ...), custom_call_target="tpu_custom_call" | custom-call | tf_op jit(solution)/shard_map/layer/pallas_call | solution.py:292
  94.7 1.4 %copy.12 = bf16[1,4,3584]{2,1,0:T(4,128)(2,1)} copy(bf16[1,4,3584]{2,1,0:T(4,128)(2,1)} %bitcast.15) | data formatting | bytes 57344

commit v5 on v4

--- a/solution.py
+++ b/solution.py
@@ -13,7 +13,7 @@
 BLOCK = 128
 NEG = -1e30
 MESH = pl.DeviceIdType.MESH
-STREAMS = 4
+STREAMS = 2
 ANY = pl.BlockSpec(memory_space=pl.ANY)
 VMEM = pl.BlockSpec(memory_space=pltpu.VMEM)
 SMEM = pl.BlockSpec(memory_space=pltpu.SMEM)
@@ -28,7 +28,7 @@
 def layer_kernel(
     slots, label_ref, mask_ref, gain_ref, q_any, k_any, v_any, res_any, wg_any, wu_any, wd_any,
     out_ref, q_ref, kv_ref, res_ref, bias, tops, sums, mid, normed, wg, wu, wd, part,
-    buf, fin, tw_in, tw_out, lsem, ksem, kssem, krsem, ssem, rsem, tsem, known,
+    pair, buf, fin, tw_in, tw_out, lsem, ksem, kssem, krsem, yssem, yrsem, ssem, rsem, tsem, known,
 ):
     rows, width = q_ref.shape
     count = kv_ref.shape[2]
@@ -36,7 +36,8 @@
     group = heads // KV_HEADS
     here = rows // BLOCK
     slot = rows // slots
-    cols = width // STREAMS
+    share = width // 2
+    cols = share // STREAMS
     c = lax.axis_index("ctx")
     first = c * here
     e = lax.axis_index("exp")
@@ -212,20 +213,45 @@
         way, farthest, _ = plan[i]
         return (z + way * (farthest - step) + 2 * slots) % slots
 
+    side = e % 2
+    mine_at = pl.multiple_of(side * share, HEAD_DIM)
+    lengths = [farthest - nearest + 1 for _, farthest, nearest in plan]
+    ahead = 3
+
+    def across(i, step):
+        at = z if i == len(plan) else chunk(i, step)
+        return pltpu.make_async_remote_copy(
+            src_ref=part.at[at, :, pl.ds(pl.multiple_of((1 - side) * share, HEAD_DIM), share)],
+            dst_ref=pair.at[at],
+            send_sem=yssem.at[i, step],
+            recv_sem=yrsem.at[i, step],
+            device_id={"exp": twin},
+            device_id_type=MESH,
+        )
+
+    def across_all(step):
+        for i in range(len(plan)):
+            if step < lengths[i]:
+                across(i, step).start()
+
     def advance(i, step, t):
         at = pl.ds(t * cols, cols)
-        src = buf.at[i, step - 1, :, at]
-        hop(i, step - 1, t, src).wait_recv()
-        own = part[chunk(i, step), :, at]
-        buf[i, step - 1, :, at] = (buf[i, step - 1, :, at].astype(jnp.float32) + own.astype(jnp.float32)).astype(
-            jnp.bfloat16
-        )
+        c_at = chunk(i, step)
+        if t == 0:
+            across(i, step).wait_recv()
+        value = part[c_at, :, pl.ds(pl.multiple_of(mine_at + t * cols, HEAD_DIM), cols)].astype(jnp.float32)
+        value = value + pair[c_at, :, at].astype(jnp.float32)
+        src = pair.at[c_at, :, at]
+        if step > 0:
+            hop(i, step - 1, t, src).wait_recv()
+            value = value + buf[i, step - 1, :, at].astype(jnp.float32)
+        pair[c_at, :, at] = value.astype(jnp.bfloat16)
         hop(i, step, t, src).start()
 
     section = jnp.where(e >= slots, 1, 0)
     tile = width // 4
     for u in range(4):
-        span = slice(u * tile, (u + 1) * tile)
+        span = pl.ds(pl.multiple_of(((2 - 2 * side + u) % 4) * tile, HEAD_DIM), tile)
         out = jnp.dot(hidden, wd[:, span], preferred_element_type=jnp.float32)
         for b in range(here):
             keep = label_ref[first + b] == section
@@ -233,44 +259,44 @@
             part[b * (BLOCK // slot):(b + 1) * (BLOCK // slot), :, span] = kept.reshape(
                 BLOCK // slot, slot, tile
             ).astype(jnp.bfloat16)
-        for t in range(STREAMS):
-            if (u + 1) * STREAMS == 4 * (t + 1):
-                for i in range(len(plan)):
-                    hop(i, 0, t, part.at[chunk(i, 0), :, pl.ds(t * cols, cols)]).start()
-
-    lengths = [farthest - nearest + 1 for _, farthest, nearest in plan]
-    same = min(lengths) - 1
-
-    def step_all(step, carry):
-        for t in range(STREAMS):
-            for i in range(len(plan)):
-                advance(i, step, t)
-        return carry
-
-    if same > 1:
-        lax.fori_loop(1, same, step_all, 0)
-    for step in range(max(same, 1), max(lengths)):
+        if u == 1:
+            for step in range(ahead):
+                across_all(step)
+    for step in range(max(lengths)):
+        across_all(step + ahead)
+        if step + ahead == max(max(lengths) - 1, ahead):
+            across(len(plan), 0).start()
         for t in range(STREAMS):
             for i in range(len(plan)):
                 if step < lengths[i]:
                     advance(i, step, t)
-    mine = part[z].astype(jnp.float32)
+    across(len(plan), 0).wait_recv()
+    mine = part[z, :, pl.ds(mine_at, share)].astype(jnp.float32) + pair[z].astype(jnp.float32)
     for i in (2, 3, 0, 1):
         for t in range(STREAMS):
             at = pl.ds(t * cols, cols)
             hop(i, lengths[i] - 1, t, fin.at[i, :, at]).wait_recv()
         mine = mine + fin[i].astype(jnp.float32)
-    tw_out[...] = mine.astype(jnp.bfloat16)
+    tw_out[...] = mine
     swap = pltpu.make_async_remote_copy(
         src_ref=tw_out, dst_ref=tw_in, send_sem=tsem.at[0], recv_sem=tsem.at[1],
         device_id={"exp": twin}, device_id_type=MESH,
     )
     swap.start()
+    size = slot // 2
+
+    def put(start, value):
+        total = mid[pl.ds(pl.multiple_of(z * slot, slot), slot), pl.ds(start, share)] + value
+        out_ref[:, pl.ds(start, share)] = jnp.where(side == 0, total[:size], total[size:]).astype(jnp.bfloat16)
+
+    put(mine_at, mine)
     swap.wait_recv()
-    total = mid[pl.ds(pl.multiple_of(z * slot, slot), slot), :] + (mine + tw_in[...].astype(jnp.float32))
-    size = slot // 2
-    out_ref[...] = jnp.where(e % 2 == 0, total[:size], total[size:]).astype(jnp.bfloat16)
+    put(pl.multiple_of((1 - side) * share, HEAD_DIM), tw_in[...])
     swap.wait_send()
+    across(len(plan), 0).wait_send()
+    for i in range(len(plan)):
+        for step in range(lengths[i]):
+            across(i, step).wait_send()
     for stage in range(3):
         for kind in range(2):
             for g in range(KV_HEADS):
@@ -278,7 +304,7 @@
     for i in range(len(plan)):
         for step in range(lengths[i]):
             for t in range(STREAMS):
-                hop(i, step, t, part.at[0, :, pl.ds(t * cols, cols)]).wait_send()
+                hop(i, step, t, pair.at[0, :, pl.ds(t * cols, cols)]).wait_send()
 
 
 def layer(labels, mask, q, k, v, res, gains, wg, wu, wd, exp_count):
@@ -307,14 +333,17 @@
             pltpu.VMEM((hidden, width), half),
             pltpu.VMEM((hidden, width), half),
             pltpu.VMEM((slots, slot, width), half),
-            pltpu.VMEM((4, steps, slot, width), half),
-            pltpu.VMEM((4, slot, width), half),
-            pltpu.VMEM((slot, width), half),
-            pltpu.VMEM((slot, width), half),
+            pltpu.VMEM((slots, slot, width // 2), half),
+            pltpu.VMEM((4, steps, slot, width // 2), half),
+            pltpu.VMEM((4, slot, width // 2), half),
+            pltpu.VMEM((slot, width // 2), jnp.float32),
+            pltpu.VMEM((slot, width // 2), jnp.float32),
             pltpu.SemaphoreType.DMA((5,)),
             pltpu.SemaphoreType.DMA((2, KV_HEADS)),
             pltpu.SemaphoreType.DMA((3, 2, KV_HEADS)),
             pltpu.SemaphoreType.DMA((3, 2, KV_HEADS)),
+            pltpu.SemaphoreType.DMA((5, steps)),
+            pltpu.SemaphoreType.DMA((5, steps)),
             pltpu.SemaphoreType.DMA((4, steps, STREAMS)),
             pltpu.SemaphoreType.DMA((4, steps, STREAMS)),
             pltpu.SemaphoreType.DMA((2,)),

time: 96.3 us -> 89.8 us (0.933)
  the two profiles are of different devices: /device:TPU:70 before, /device:TPU:4 now
where the time goes in v5:
time: 89.8 us; the launch traced here: 89.5 us
  Pallas kernels  88.2 us (98%)
  local copies, waits for them, and re-layouts  1.37 us (2%)
    pallas_call x1, Pallas kernels, layer(): pl.pallas_call(functools.partial(layer_kernel, slots), out_shape=jax.Shap...  88.2 us

profile of v5, /device:TPU:4, one launch (start us, length us, event | category | flops | bytes accessed | tf_op | source)
XLA Modules:
  0.0 89.5 jit_solution(8743847118790637944)
XLA Ops:
  0.0 88.2 %layer.1 = bf16[4,3584]{1,0:T(4,128)(2,1)} custom-call(s32[8]{0:T(128)} %bitcast.17, s32[8,8]{1,0:T(8,128)} %bitcast.16, f32[2,3584]{1,0:T(2,128)} %gain_ref.1, bf16[256,3584]{1,0:T(8,128)(2,1)} %bitcast.11, bf16[256,512]{1,0:T(8,128)(2,1)} %bitcast.13, bf16[256,512]{1,0:T(8,128)(2,1)} %bitcast.14, bf16[256,3584]{1,0:T(8,128)(2,1)} %bitcast.12, ...), custom_call_target="tpu_custom_call" | custom-call | tf_op jit(solution)/shard_map/layer/pallas_call | solution.py:318
  88.2 1.4 %copy.12 = bf16[1,4,3584]{2,1,0:T(4,128)(2,1)} copy(bf16[1,4,3584]{2,1,0:T(4,128)(2,1)} %bitcast.15) | data formatting | bytes 57344

commit v6 on v5

--- a/solution.py
+++ b/solution.py
@@ -116,12 +116,16 @@
             pl.semaphore_signal(known.at[i], inc=1, device_id={"exp": along(way)}, device_id_type=MESH)
 
     def learn(i):
-        pl.semaphore_wait(known.at[i], 2)
+        if i < len(hops):
+            pl.semaphore_wait(known.at[i], 2)
+        if i + 1 < len(hops):
+            tell(i + 1, hops[i + 1])
 
     hops, distance = [], 1
     while distance < reach:
         hops.append(min(distance, reach - distance))
         distance += hops[-1]
+    assert len(hops) <= 4
     tell(0, hops[0])
     for load in loads[:2]:
         load.wait()
@@ -147,7 +151,10 @@
         )
         return carry
 
-    lax.fori_loop(0, heads, begin, 0, unroll=4)
+    early = heads // 2
+    lax.fori_loop(0, early, begin, 0, unroll=min(early, 7))
+    learn(0)
+    lax.fori_loop(early, heads, begin, 0, unroll=min(early, 7))
 
     def finish(g, h, squares):
         rest = slice(rows, count)
@@ -177,10 +184,8 @@
         for stage in (1, 2):
             for kind in range(2):
                 piece(stage, kind, g).wait_recv()
-        if g < len(hops):
-            learn(g)
-            if g + 1 < len(hops):
-                tell(g + 1, hops[g + 1])
+        if g in (0, 2):
+            learn(1 + g // 2)
         squares = lax.fori_loop(g * group, (g + 1) * group, functools.partial(finish, g), squares, unroll=group)
     inverse = lax.rsqrt(jnp.sum(squares, axis=-1, keepdims=True) / width + 1e-05)
     for b in range(here):
@@ -248,6 +253,7 @@
         pair[c_at, :, at] = value.astype(jnp.bfloat16)
         hop(i, step, t, src).start()
 
+    learn(3)
     section = jnp.where(e >= slots, 1, 0)
     tile = width // 4
     for u in range(4):

time: 89.8 us -> 89.3 us (level)
  no operation moved by 1% of the time
where the time goes in v6:
time: 89.3 us; the launch traced here: 89 us
  Pallas kernels  87.7 us (98%)
  local copies, waits for them, and re-layouts  1.37 us (2%)
    pallas_call x1, Pallas kernels, layer(): pl.pallas_call(functools.partial(layer_kernel, slots), out_shape=jax.Shap...  87.7 us

profile of v6, /device:TPU:4, one launch (start us, length us, event | category | flops | bytes accessed | tf_op | source)
XLA Modules:
  0.0 89.0 jit_solution(6693391976532860862)
XLA Ops:
  0.0 87.7 %layer.1 = bf16[4,3584]{1,0:T(4,128)(2,1)} custom-call(s32[8]{0:T(128)} %bitcast.17, s32[8,8]{1,0:T(8,128)} %bitcast.16, f32[2,3584]{1,0:T(2,128)} %gain_ref.1, bf16[256,3584]{1,0:T(8,128)(2,1)} %bitcast.11, bf16[256,512]{1,0:T(8,128)(2,1)} %bitcast.13, bf16[256,512]{1,0:T(8,128)(2,1)} %bitcast.14, bf16[256,3584]{1,0:T(8,128)(2,1)} %bitcast.12, ...), custom_call_target="tpu_custom_call" | custom-call | tf_op jit(solution)/shard_map/layer/pallas_call | solution.py:324
  87.7 1.4 %copy.12 = bf16[1,4,3584]{2,1,0:T(4,128)(2,1)} copy(bf16[1,4,3584]{2,1,0:T(4,128)(2,1)} %bitcast.15) | data formatting | bytes 57344

commit v7 on v6

--- a/solution.py
+++ b/solution.py
@@ -21,7 +21,7 @@
 
 def chains(slots):
     half = slots // 2
-    near = half // 2 + half // 16
+    near = half // 2
     return ((1, half - 1, near + 1), (-1, half, near + 1), (1, near, 1), (-1, near, 1))
 
 
@@ -283,7 +283,7 @@
             at = pl.ds(t * cols, cols)
             hop(i, lengths[i] - 1, t, fin.at[i, :, at]).wait_recv()
         mine = mine + fin[i].astype(jnp.float32)
-    tw_out[...] = mine
+    tw_out[...] = mine.astype(jnp.bfloat16)
     swap = pltpu.make_async_remote_copy(
         src_ref=tw_out, dst_ref=tw_in, send_sem=tsem.at[0], recv_sem=tsem.at[1],
         device_id={"exp": twin}, device_id_type=MESH,
@@ -297,7 +297,7 @@
 
     put(mine_at, mine)
     swap.wait_recv()
-    put(pl.multiple_of((1 - side) * share, HEAD_DIM), tw_in[...])
+    put(pl.multiple_of((1 - side) * share, HEAD_DIM), tw_in[...].astype(jnp.float32))
     swap.wait_send()
     across(len(plan), 0).wait_send()
     for i in range(len(plan)):
@@ -342,8 +342,8 @@
             pltpu.VMEM((slots, slot, width // 2), half),
             pltpu.VMEM((4, steps, slot, width // 2), half),
             pltpu.VMEM((4, slot, width // 2), half),
-            pltpu.VMEM((slot, width // 2), jnp.float32),
-            pltpu.VMEM((slot, width // 2), jnp.float32),
+            pltpu.VMEM((slot, width // 2), half),
+            pltpu.VMEM((slot, width // 2), half),
             pltpu.SemaphoreType.DMA((5,)),
             pltpu.SemaphoreType.DMA((2, KV_HEADS)),
             pltpu.SemaphoreType.DMA((3, 2, KV_HEADS)),

time: 89.3 us -> 90.6 us (1.015)
  Pallas kernels: 87.7 us -> 88.9 us
    pallas_call x1, Pallas kernels: 87.7 us -> 88.9 us  [layer(): pl.pallas_call(functools.partial(layer_kernel, slots), out_shape=jax.Shap...]
where the time goes in v7:
time: 90.6 us; the launch traced here: 90.2 us
  Pallas kernels  88.9 us (98%)
  local copies, waits for them, and re-layouts  1.37 us (2%)
    pallas_call x1, Pallas kernels, layer(): pl.pallas_call(functools.partial(layer_kernel, slots), out_shape=jax.Shap...  88.9 us

profile of v7, /device:TPU:4, one launch (start us, length us, event | category | flops | bytes accessed | tf_op | source)
XLA Modules:
  0.0 90.2 jit_solution(9454563303345505451)
XLA Ops:
  0.0 88.9 %layer.1 = bf16[4,3584]{1,0:T(4,128)(2,1)} custom-call(s32[8]{0:T(128)} %bitcast.17, s32[8,8]{1,0:T(8,128)} %bitcast.16, f32[2,3584]{1,0:T(2,128)} %gain_ref.1, bf16[256,3584]{1,0:T(8,128)(2,1)} %bitcast.11, bf16[256,512]{1,0:T(8,128)(2,1)} %bitcast.13, bf16[256,512]{1,0:T(8,128)(2,1)} %bitcast.14, bf16[256,3584]{1,0:T(8,128)(2,1)} %bitcast.12, ...), custom_call_target="tpu_custom_call" | custom-call | tf_op jit(solution)/shard_map/layer/pallas_call | solution.py:324
  88.9 1.4 %copy.12 = bf16[1,4,3584]{2,1,0:T(4,128)(2,1)} copy(bf16[1,4,3584]{2,1,0:T(4,128)(2,1)} %bitcast.15) | data formatting | bytes 57344
